TPU v7x, 256 devices: a whole 4x4x8 slice. The times are simulated.
256 devices in a mesh: gx: 16 (over x, y), gy: 2 (over core), gz: 8 (over z).
Axes of the slice: x: 4, y: 4, z: 8, core: 2. Of those that a mesh axis runs over, the one named last changes fastest.
Arguments:
- field: float32 [2, 1024, 128, 1024], P(None, 'gx', 'gy', 'gz'), as said below
- start_basis: float32 [1024, 256], replicated, may hold values from -6 to 6
Outputs:
- factor: float32 [1024, 256], P('gx')
- core: float32 [2, 256, 128, 1024], P(None, 'gx', 'gy', 'gz')
Inputs may be any that keep to these rules, and one draw needn't show every extreme that they name: Real-valued field; no structure is promised.
All inputs are finite; a program needn't handle non-finite values.
Results may differ from a plain program's by a relative error of at most 0.0002.
Values sent between devices are 32-bit elements; how exact they have to be, the bound alone decides.
A program may use at most 64 MiB of HBM per device.

v0:
```python
import jax
import jax.numpy as jnp
from jax import lax
from jax.sharding import PartitionSpec as P

ITERS = 2


def orthonormal(image):
    small = jnp.dot(image.T, image, precision=lax.Precision.HIGHEST)
    lower = jnp.linalg.cholesky(small)
    return jax.scipy.linalg.solve_triangular(lower, image.T, lower=True).T


def per_device(field, start_basis):
    comps, slab, cells_y, cells_z = field.shape
    flat_field = field.reshape(comps, slab, cells_y * cells_z)
    fibers = lax.all_to_all(flat_field, "gx", split_axis=2, concat_axis=1, tiled=True)
    basis = start_basis
    local_gram = jnp.einsum("crm,csm->rs", fibers, fibers, precision=lax.Precision.HIGHEST)
    gram = lax.psum(local_gram, ("gx", "gy", "gz"))
    for step in range(ITERS):
        image = jnp.dot(gram, basis, precision=lax.Precision.HIGHEST)
        basis = orthonormal(image)
    projected = jnp.einsum("rk,crm->ckm", basis, fibers, precision=lax.Precision.HIGHEST)
    returned = lax.all_to_all(projected, "gx", split_axis=1, concat_axis=2, tiled=True)
    offset = lax.axis_index("gx") * slab
    factor = lax.dynamic_slice_in_dim(basis, offset, slab, 0)
    return (factor, returned.reshape(comps, returned.shape[1], cells_y, cells_z))


def solution(mesh):
    placed = (P(None, "gx", "gy", "gz"), P())
    return jax.shard_map(
        per_device,
        mesh=mesh,
        in_specs=placed,
        out_specs=(P("gx", None), P(None, "gx", "gy", "gz")),
        check_vma=False,
    )
```

profile of v0, /device:TPU:97, one launch (start us, length us, event | category | flops | bytes accessed | tf_op | source)
XLA Modules:
  0.0 604.0 jit_solution(12621777568615691695)
XLA Ops:
  7.2 8.4 %copy.13 = f32[2,64,64,128]{1,0,3,2:T(2,128)} copy(f32[2,64,64,128]{3,2,1,0:T(8,128)} %param.5) | data formatting | bytes 8388608 | tf_op args[0]
  15.7 15.1 %reshape.52 = f32[16,1,65536]{2,1,0:T(1,128)} reshape(f32[8192,2,64]{2,1,0:T(2,128)} %bitcast.97) | data formatting | bytes 8388608
  30.8 56.1 %all_to_all.33 = f32[16,1,65536]{2,1,0:T(1,128)} all-to-all(f32[16,1,65536]{2,1,0:T(1,128)} %reshape.52), channel_id=1, replica_groups=mesh['gx'=16,'gy'=2,'gz'=8] {'gx'}, dimensions={0} | all-to-all | bytes 8388608 | tf_op jit(solution)/shard_map/all_to_all | solution.py:18
  87.3 13.7 %reduce.8 = f32[16,65536]{1,0:T(8,128)} reduce(f32[16,1,65536]{2,1,0:T(1,128)} %all_to_all.33, f32[]{:T(128)} %broadcast.87), dimensions={1}, to_apply=%all_to_all.24.reduce_sub_computation | reduce | bytes 8388612 | tf_op jit(solution)/shard_map/all_to_all | solution.py:18
  101.0 9.7 %reshape.53 = f32[8192,2,64]{2,1,0:T(2,128)} reshape(f32[16,65536]{1,0:T(8,128)} %reduce.8) | data formatting | bytes 8388608
  110.7 12.2 %copy.26 = f32[2,64,16,512]{3,1,2,0:T(8,128)} copy(f32[2,64,16,512]{1,0,3,2:T(2,128)} %bitcast.96) | data formatting | bytes 8388608 | tf_op jit(solution)/shard_map/all_to_all | solution.py:18
  122.9 17.6 %convolution_bitcast_fusion = f32[1024,1024]{1,0:T(8,128)} fusion(f32[2,1024,512]{2,1,0:T(8,128)} %bitcast.98), kind=kOutput, calls=%fused_computation.4 | convolution fusion | flops 12884901888 | bytes 8388608 | tf_op jit(solution)/shard_map/crm,csm->rs/dot_general | solution.py:20
  140.6 270.4 %all-reduce.3.cloned.1.call-done = f32[1024,1024]{1,0:T(8,128)} async-done(((f32[1024,1024]{1,0:T(8,128)}), f32[1024,1024]{1,0:T(8,128)}) %all-reduce.3.cloned.1.call-update) | async-done | bytes 4194320 | tf_op jit(solution)/shard_map/psum | solution.py:21
  411.0 5.5 fusion.32
  416.5 1.8 fusion.33
  418.5 11.7 %cholesky.130 = f32[128,128]{1,0:T(8,128)S(1)} custom-call(f32[128,128]{1,0:T(8,128)S(1)} %cholesky.194), custom_call_target="Cholesky" | custom-call | tf_op jit(solution)/shard_map/jit(cholesky)/cholesky | solution.py:11
  430.3 9.8 %custom-call.13 = f32[1,128,128]{1,2,0:T(8,128)S(1)} custom-call(f32[1,128,128]{2,1,0:T(8,128)S(1)} %get-tuple-element.53), custom_call_target="InvertDiagBlocksLowerTriangular" | custom-call | tf_op jit(solution)/shard_map/jit(cholesky)/cholesky | solution.py:11
  440.6 11.7 %cholesky.147 = f32[128,128]{1,0:T(8,128)S(1)} custom-call(f32[128,128]{1,0:T(8,128)S(1)} %convolution_subtract_fusion.3), custom_call_target="Cholesky" | custom-call | tf_op jit(solution)/shard_map/jit(cholesky)/cholesky | solution.py:11
  467.2 3.9 while.4
  471.2 19.7 %custom-call.14 = f32[2,128,128]{1,2,0:T(8,128)S(1)} custom-call(f32[2,128,128]{2,1,0:T(8,128)S(1)} %get-tuple-element.18), custom_call_target="InvertDiagBlocksLowerTriangular" | custom-call | tf_op jit(solution)/shard_map/jit(_solve_triangular)/triangular_solve | solution.py:12
  493.2 5.3 fusion.2
  500.5 11.7 %cholesky.164 = f32[128,128]{1,0:T(8,128)S(1)} custom-call(f32[128,128]{1,0:T(8,128)S(1)} %cholesky.197), custom_call_target="Cholesky" | custom-call | tf_op jit(solution)/shard_map/jit(cholesky)/cholesky | solution.py:11
  512.3 9.8 %custom-call.15 = f32[1,128,128]{1,2,0:T(8,128)S(1)} custom-call(f32[1,128,128]{2,1,0:T(8,128)S(1)} %get-tuple-element.49), custom_call_target="InvertDiagBlocksLowerTriangular" | custom-call | tf_op jit(solution)/shard_map/jit(cholesky)/cholesky | solution.py:11
  522.6 11.7 %cholesky.181 = f32[128,128]{1,0:T(8,128)S(1)} custom-call(f32[128,128]{1,0:T(8,128)S(1)} %convolution_subtract_fusion.2), custom_call_target="Cholesky" | custom-call | tf_op jit(solution)/shard_map/jit(cholesky)/cholesky | solution.py:11
  537.2 4.0 while.5
  541.2 19.7 %custom-call.16 = f32[2,128,128]{1,2,0:T(8,128)S(1)} custom-call(f32[2,128,128]{2,1,0:T(8,128)S(1)} %get-tuple-element.19), custom_call_target="InvertDiagBlocksLowerTriangular" | custom-call | tf_op jit(solution)/shard_map/jit(_solve_triangular)/triangular_solve | solution.py:12
  563.2 5.7 convolution_bitcast_fusion.1
  570.7 4.6 all-to-all-start.1
  576.1 17.8 %all-to-all-done.1 = f32[2,256,512]{2,0,1:T(2,128)} async-done(((f32[2,256,512]{2,0,1:T(2,128)}), f32[2,256,512]{2,0,1:T(2,128)}, u32[]{:S(2)}, u32[]{:S(2)}) %all-to-all-start.1) | async-done | bytes 1048608 | tf_op jit(solution)/shard_map/all_to_all | solution.py:26
  (54 shorter events, 24.0 us)
Async XLA Ops:
  7.2 403.9 %copy-start = (f32[1024,256]{1,0:T(8,128)S(1)}, f32[1024,256]{1,0:T(8,128)}, u32[]{:S(2)}) copy-start(f32[1024,256]{1,0:T(8,128)} %param.6) | copy-start | bytes 3145732
  7.2 403.8 %all-reduce.3.cloned.1.call-start = ((), (), s32[]{:S(2)}) async-start(), calls=%async_computation.2 | async-start | bytes 8388608 | tf_op jit(solution)/shard_map/psum | solution.py:21
  570.7 23.2 %all-to-all-start.1 = ((f32[2,256,512]{2,0,1:T(2,128)}), f32[2,256,512]{2,0,1:T(2,128)}, u32[]{:S(2)}, u32[]{:S(2)}) async-start(f32[2,256,512]{2,0,1:T(2,128)} %copy.20), calls=%async_computation.1 | async-start | bytes 2097152 | tf_op jit(solution)/shard_map/all_to_all | solution.py:26
Sparse Core Ops, SparseCore 0:
  140.7 270.2 all-reduce.2
where the time goes:
time: 614 us; the launch traced here: 604 us
  waiting for transfers between devices  288 us (47%)
  other arithmetic  122 us (20%)
  local copies, waits for them, and re-layouts  59.5 us (10%)
  blocking collectives  56.1 us (9%)
  matrix products  43.3 us (7%)
  between operations  30.1 us (5%)
    psum x1, waiting for transfers between devices, per_device(): gram = lax.psum(local_gram, ('gx', 'gy', 'gz'))  270 us
    another operation x13, other arithmetic, orthonormal(): lower = jnp.linalg.cholesky(small)  68.5 us
    all_to_all x1, blocking collectives, per_device(): lax.all_to_all(flat_field, 'gx', split_axis=2, concat_axis=1, tiled=True)  56.1 us
    another operation x5, other arithmetic, orthonormal(): return jax.scipy.linalg.solve_triangular(lower, image.T, lower=True).T  39.6 us
    unnamed x6, local copies, waits for them, and re-layouts  33.9 us
    all_to_all x1, waiting for transfers between devices, per_device(): lax.all_to_all(projected, 'gx', split_axis=1, concat_axis=2, tiled=True)  17.8 us
    dot_general x1, matrix products, per_device(): jnp.einsum('crm,csm->rs', fibers, fibers, precision=lax.Precision.HIGHEST)  17.6 us
    all_to_all x1, other arithmetic, per_device(): lax.all_to_all(flat_field, 'gx', split_axis=2, concat_axis=1, tiled=True)  13.7 us
  transfers between devices with their start and end apart: 2, of which 2 were waited for; matrix products, arithmetic and copies ran while one was open for 0% of the time, Pallas kernels for 0%

commit v1 on v0

--- a/solution.py
+++ b/solution.py
@@ -4,6 +4,30 @@
 from jax.sharding import PartitionSpec as P
 
 ITERS = 2
+
+
+def cut_along(x, dim, size):
+    shape = x.shape
+    tiles = x.reshape(*shape[:dim], size, shape[dim] // size, *shape[dim + 1 :])
+    return jnp.moveaxis(tiles, dim, 0)
+
+
+def laid_out(blocks, dim):
+    blocks = jnp.moveaxis(blocks, 0, dim)
+    shape = blocks.shape
+    return blocks.reshape(*shape[:dim], shape[dim] * shape[dim + 1], *shape[dim + 2 :])
+
+
+def rotated_exchange(x, axis, split_dim, concat_dim):
+    size, place = (lax.axis_size(axis), lax.axis_index(axis))
+    pieces = cut_along(x, split_dim, size)
+    whole = pieces
+    for step in range(1, size):
+        target, source = ((place + step) % size, (place - step) % size)
+        sent = lax.dynamic_index_in_dim(pieces, target, 0)
+        other = lax.ppermute(sent, axis, [(i, (i + step) % size) for i in range(size)])
+        whole = lax.dynamic_update_slice_in_dim(whole, other, source, axis=0)
+    return laid_out(whole, concat_dim)
 
 
 def orthonormal(image):
@@ -23,7 +47,7 @@
         image = jnp.dot(gram, basis, precision=lax.Precision.HIGHEST)
         basis = orthonormal(image)
     projected = jnp.einsum("rk,crm->ckm", basis, fibers, precision=lax.Precision.HIGHEST)
-    returned = lax.all_to_all(projected, "gx", split_axis=1, concat_axis=2, tiled=True)
+    returned = rotated_exchange(projected, "gx", 1, 2)
     offset = lax.axis_index("gx") * slab
     factor = lax.dynamic_slice_in_dim(basis, offset, slab, 0)
     return (factor, returned.reshape(comps, returned.shape[1], cells_y, cells_z))

time: 614 us -> 612 us (level)
  the two profiles are of different devices: /device:TPU:97 before, /device:TPU:24 now
where the time goes in v1:
time: 612 us; the launch traced here: 602 us
  waiting for transfers between devices  276 us (45%)
  other arithmetic  122 us (20%)
  local copies, waits for them, and re-layouts  57 us (9%)
  blocking collectives  56.1 us (9%)
  matrix products  43.5 us (7%)
  starting transfers between devices  29 us (5%)
  between operations  18.1 us (3%)
    psum x1, waiting for transfers between devices, per_device(): gram = lax.psum(local_gram, ('gx', 'gy', 'gz'))  270 us
    another operation x13, other arithmetic, orthonormal(): lower = jnp.linalg.cholesky(small)  68.6 us
    all_to_all x1, blocking collectives, per_device(): lax.all_to_all(flat_field, 'gx', split_axis=2, concat_axis=1, tiled=True)  56.1 us
    another operation x5, other arithmetic, orthonormal(): return jax.scipy.linalg.solve_triangular(lower, image.T, lower=True).T  39.8 us
    unnamed x6, local copies, waits for them, and re-layouts  33.9 us
    ppermute x15, starting transfers between devices, rotated_exchange(): lax.ppermute(sent, axis, [(i, (i + step) % size) for i in range(size)])  28.9 us
    dot_general x1, matrix products, per_device(): jnp.einsum('crm,csm->rs', fibers, fibers, precision=lax.Precision.HIGHEST)  18.1 us
    all_to_all x1, other arithmetic, per_device(): lax.all_to_all(flat_field, 'gx', split_axis=2, concat_axis=1, tiled=True)  13.7 us
  transfers between devices with their start and end apart: 16, of which 4 were waited for; matrix products, arithmetic and copies ran while one was open for 0% of the time, Pallas kernels for 0%

profile of v1, /device:TPU:24, one launch (start us, length us, event | category | flops | bytes accessed | tf_op | source)
XLA Modules:
  0.0 602.0 jit_solution(6911518079677584891)
XLA Ops:
  7.2 8.4 %copy.13 = f32[2,64,64,128]{1,0,3,2:T(2,128)} copy(f32[2,64,64,128]{3,2,1,0:T(8,128)} %param.5) | data formatting | bytes 8388608 | tf_op args[0]
  15.7 15.1 %reshape.66 = f32[16,1,65536]{2,1,0:T(1,128)} reshape(f32[8192,2,64]{2,1,0:T(2,128)} %bitcast.128) | data formatting | bytes 8388608
  30.8 56.1 %all_to_all.18 = f32[16,1,65536]{2,1,0:T(1,128)} all-to-all(f32[16,1,65536]{2,1,0:T(1,128)} %reshape.66), channel_id=1, replica_groups=mesh['gx'=16,'gy'=2,'gz'=8] {'gx'}, dimensions={0} | all-to-all | bytes 8388608 | tf_op jit(solution)/shard_map/all_to_all | solution.py:42
  87.4 13.7 %reduce.8 = f32[16,65536]{1,0:T(8,128)} reduce(f32[16,1,65536]{2,1,0:T(1,128)} %all_to_all.18, f32[]{:T(128)} %broadcast.117), dimensions={1}, to_apply=%all_to_all.13.reduce_sub_computation | reduce | bytes 8388612 | tf_op jit(solution)/shard_map/all_to_all | solution.py:42
  101.1 9.7 %reshape.67 = f32[8192,2,64]{2,1,0:T(2,128)} reshape(f32[16,65536]{1,0:T(8,128)} %reduce.8) | data formatting | bytes 8388608
  110.7 12.2 %copy.25 = f32[2,64,16,512]{3,1,2,0:T(8,128)} copy(f32[2,64,16,512]{1,0,3,2:T(2,128)} %bitcast.127) | data formatting | bytes 8388608 | tf_op jit(solution)/shard_map/all_to_all | solution.py:42
  122.9 18.1 %convolution_bitcast_fusion = f32[1024,1024]{1,0:T(8,128)} fusion(f32[2,1024,512]{2,1,0:T(8,128)} %bitcast.129), kind=kOutput, calls=%fused_computation.4 | convolution fusion | flops 12884901888 | bytes 8388608 | tf_op jit(solution)/shard_map/crm,csm->rs/dot_general | solution.py:44
  141.6 269.7 %all-reduce.3.cloned.1.call-done = f32[1024,1024]{1,0:T(8,128)} async-done(((f32[1024,1024]{1,0:T(8,128)}), f32[1024,1024]{1,0:T(8,128)}) %all-reduce.3.cloned.1.call-update) | async-done | bytes 4194320 | tf_op jit(solution)/shard_map/psum | solution.py:45
  411.4 5.2 fusion.33
  418.6 11.7 %cholesky.130 = f32[128,128]{1,0:T(8,128)S(1)} custom-call(f32[128,128]{1,0:T(8,128)S(1)} %cholesky.194), custom_call_target="Cholesky" | custom-call | tf_op jit(solution)/shard_map/jit(cholesky)/cholesky | solution.py:35
  430.4 9.8 %custom-call.13 = f32[1,128,128]{1,2,0:T(8,128)S(1)} custom-call(f32[1,128,128]{2,1,0:T(8,128)S(1)} %get-tuple-element.68), custom_call_target="InvertDiagBlocksLowerTriangular" | custom-call | tf_op jit(solution)/shard_map/jit(cholesky)/cholesky | solution.py:35
  440.7 11.7 %cholesky.147 = f32[128,128]{1,0:T(8,128)S(1)} custom-call(f32[128,128]{1,0:T(8,128)S(1)} %convolution_subtract_fusion.3), custom_call_target="Cholesky" | custom-call | tf_op jit(solution)/shard_map/jit(cholesky)/cholesky | solution.py:35
  454.8 4.1 while.4
  458.9 19.7 %custom-call.14 = f32[2,128,128]{1,2,0:T(8,128)S(1)} custom-call(f32[2,128,128]{2,1,0:T(8,128)S(1)} %get-tuple-element.18), custom_call_target="InvertDiagBlocksLowerTriangular" | custom-call | tf_op jit(solution)/shard_map/jit(_solve_triangular)/triangular_solve | solution.py:36
  480.9 5.3 fusion.3
  488.3 11.7 %cholesky.164 = f32[128,128]{1,0:T(8,128)S(1)} custom-call(f32[128,128]{1,0:T(8,128)S(1)} %cholesky.197), custom_call_target="Cholesky" | custom-call | tf_op jit(solution)/shard_map/jit(cholesky)/cholesky | solution.py:35
  500.1 9.8 %custom-call.15 = f32[1,128,128]{1,2,0:T(8,128)S(1)} custom-call(f32[1,128,128]{2,1,0:T(8,128)S(1)} %get-tuple-element.64), custom_call_target="InvertDiagBlocksLowerTriangular" | custom-call | tf_op jit(solution)/shard_map/jit(cholesky)/cholesky | solution.py:35
  510.4 11.7 %cholesky.181 = f32[128,128]{1,0:T(8,128)S(1)} custom-call(f32[128,128]{1,0:T(8,128)S(1)} %convolution_subtract_fusion.2), custom_call_target="Cholesky" | custom-call | tf_op jit(solution)/shard_map/jit(cholesky)/cholesky | solution.py:35
  525.1 4.0 while.5
  529.2 19.7 %custom-call.16 = f32[2,128,128]{1,2,0:T(8,128)S(1)} custom-call(f32[2,128,128]{2,1,0:T(8,128)S(1)} %get-tuple-element.19), custom_call_target="InvertDiagBlocksLowerTriangular" | custom-call | tf_op jit(solution)/shard_map/jit(_solve_triangular)/triangular_solve | solution.py:36
  551.1 5.7 fusion.1
  562.7 4.2 collective-permute-start.4
  580.0 6.0 collective-permute-start.12
  588.5 4.8 collective-permute-done.13
  (97 shorter events, 43.8 us)
Async XLA Ops:
  7.2 404.2 %copy-start = (f32[1024,256]{1,0:T(8,128)S(1)}, f32[1024,256]{1,0:T(8,128)}, u32[]{:S(2)}) copy-start(f32[1024,256]{1,0:T(8,128)} %param.6) | copy-start | bytes 3145732
  7.2 404.2 %all-reduce.3.cloned.1.call-start = ((), (), s32[]{:S(2)}) async-start(), calls=%async_computation.1 | async-start | bytes 8388608 | tf_op jit(solution)/shard_map/psum | solution.py:45
  557.0 10.6 %collective-permute-start = (f32[1,2,16,512]{3,2,0,1:T(8,128)S(1)}, f32[1,2,16,512]{3,2,0,1:T(8,128)S(1)}, u32[]{:S(2)}, u32[]{:S(2)}) collective-permute-start(f32[1,2,16,512]{3,2,0,1:T(8,128)S(1)} %get-tuple-element.60), channel_id=1, source_target_pairs={{0,16},{16,32},{32,48},{48,64},{64,80},{80,96},{96,112},{112,128},... | collective-permute-start | bytes 196616 | tf_op jit(solution)/shard_map/ppermute | solution.py:28
  558.6 10.9 %collective-permute-start.1 = (f32[1,2,16,512]{3,2,0,1:T(8,128)S(1)}, f32[1,2,16,512]{3,2,0,1:T(8,128)S(1)}, u32[]{:S(2)}, u32[]{:S(2)}) collective-permute-start(f32[1,2,16,512]{3,2,0,1:T(8,128)S(1)} %get-tuple-element.59), channel_id=1, source_target_pairs={{0,32},{16,48},{32,64},{48,80},{64,96},{80,112},{96,128},{112,144}... | collective-permute-start | bytes 196616 | tf_op jit(solution)/shard_map/ppermute | solution.py:28
  560.6 9.3 %collective-permute-start.2 = (f32[1,2,16,512]{3,2,0,1:T(8,128)S(1)}, f32[1,2,16,512]{3,2,0,1:T(8,128)S(1)}, u32[]{:S(2)}, u32[]{:S(2)}) collective-permute-start(f32[1,2,16,512]{3,2,0,1:T(8,128)S(1)} %get-tuple-element.58), channel_id=1, source_target_pairs={{0,48},{16,64},{32,80},{48,96},{64,112},{80,128},{96,144},{112,160... | collective-permute-start | bytes 196616 | tf_op jit(solution)/shard_map/ppermute | solution.py:28
  561.5 11.7 %collective-permute-start.3 = (f32[1,2,16,512]{3,2,0,1:T(8,128)S(1)}, f32[1,2,16,512]{3,2,0,1:T(8,128)S(1)}, u32[]{:S(2)}, u32[]{:S(2)}) collective-permute-start(f32[1,2,16,512]{3,2,0,1:T(8,128)S(1)} %get-tuple-element.57), channel_id=1, source_target_pairs={{0,64},{16,80},{32,96},{48,112},{64,128},{80,144},{96,160},{112,17... | collective-permute-start | bytes 196616 | tf_op jit(solution)/shard_map/ppermute | solution.py:28
  562.7 12.7 %collective-permute-start.4 = (f32[1,2,16,512]{3,2,0,1:T(8,128)S(1)}, f32[1,2,16,512]{3,2,0,1:T(8,128)S(1)}, u32[]{:S(2)}, u32[]{:S(2)}) collective-permute-start(f32[1,2,16,512]{3,2,0,1:T(8,128)S(1)} %get-tuple-element.56), channel_id=1, source_target_pairs={{0,80},{16,96},{32,112},{48,128},{64,144},{80,160},{96,176},{112,1... | collective-permute-start | bytes 196616 | tf_op jit(solution)/shard_map/ppermute | solution.py:28
  567.7 11.4 %collective-permute-start.5 = (f32[1,2,16,512]{3,2,0,1:T(8,128)S(1)}, f32[1,2,16,512]{3,2,0,1:T(8,128)S(1)}, u32[]{:S(2)}, u32[]{:S(2)}) collective-permute-start(f32[1,2,16,512]{3,2,0,1:T(8,128)S(1)} %get-tuple-element.55), channel_id=1, source_target_pairs={{0,96},{16,112},{32,128},{48,144},{64,160},{80,176},{96,192},{112,... | collective-permute-start | bytes 196616 | tf_op jit(solution)/shard_map/ppermute | solution.py:28
  569.5 9.6 %collective-permute-start.6 = (f32[1,2,16,512]{3,2,0,1:T(8,128)S(1)}, f32[1,2,16,512]{3,2,0,1:T(8,128)S(1)}, u32[]{:S(2)}, u32[]{:S(2)}) collective-permute-start(f32[1,2,16,512]{3,2,0,1:T(8,128)S(1)} %get-tuple-element.54), channel_id=1, source_target_pairs={{0,112},{16,128},{32,144},{48,160},{64,176},{80,192},{96,208},{112... | collective-permute-start | bytes 196616 | tf_op jit(solution)/shard_map/ppermute | solution.py:28
  569.9 10.1 %collective-permute-start.7 = (f32[1,2,16,512]{3,2,0,1:T(8,128)S(1)}, f32[1,2,16,512]{3,2,0,1:T(8,128)S(1)}, u32[]{:S(2)}, u32[]{:S(2)}) collective-permute-start(f32[1,2,16,512]{3,2,0,1:T(8,128)S(1)} %get-tuple-element.53), channel_id=1, source_target_pairs={{0,128},{16,144},{32,160},{48,176},{64,192},{80,208},{96,224},{112... | collective-permute-start | bytes 196616 | tf_op jit(solution)/shard_map/ppermute | solution.py:28
  573.2 12.8 %collective-permute-start.8 = (f32[1,2,16,512]{3,2,0,1:T(8,128)S(1)}, f32[1,2,16,512]{3,2,0,1:T(8,128)S(1)}, u32[]{:S(2)}, u32[]{:S(2)}) collective-permute-start(f32[1,2,16,512]{3,2,0,1:T(8,128)S(1)} %get-tuple-element.52), channel_id=1, source_target_pairs={{0,144},{16,160},{32,176},{48,192},{64,208},{80,224},{96,240},{112... | collective-permute-start | bytes 196616 | tf_op jit(solution)/shard_map/ppermute | solution.py:28
  575.4 10.7 %collective-permute-start.9 = (f32[1,2,16,512]{3,2,0,1:T(8,128)S(1)}, f32[1,2,16,512]{3,2,0,1:T(8,128)S(1)}, u32[]{:S(2)}, u32[]{:S(2)}) collective-permute-start(f32[1,2,16,512]{3,2,0,1:T(8,128)S(1)} %get-tuple-element.51), channel_id=1, source_target_pairs={{0,160},{16,176},{32,192},{48,208},{64,224},{80,240},{96,0},{112,1... | collective-permute-start | bytes 196616 | tf_op jit(solution)/shard_map/ppermute | solution.py:28
  579.0 8.7 %collective-permute-start.10 = (f32[1,2,16,512]{3,2,0,1:T(8,128)S(1)}, f32[1,2,16,512]{3,2,0,1:T(8,128)S(1)}, u32[]{:S(2)}, u32[]{:S(2)}) collective-permute-start(f32[1,2,16,512]{3,2,0,1:T(8,128)S(1)} %get-tuple-element.50), channel_id=1, source_target_pairs={{0,176},{16,192},{32,208},{48,224},{64,240},{80,0},{96,16},{112,32... | collective-permute-start | bytes 196616 | tf_op jit(solution)/shard_map/ppermute | solution.py:28
  579.2 8.6 %collective-permute-start.11 = (f32[1,2,16,512]{3,2,0,1:T(8,128)S(1)}, f32[1,2,16,512]{3,2,0,1:T(8,128)S(1)}, u32[]{:S(2)}, u32[]{:S(2)}) collective-permute-start(f32[1,2,16,512]{3,2,0,1:T(8,128)S(1)} %get-tuple-element.49), channel_id=1, source_target_pairs={{0,192},{16,208},{32,224},{48,240},{64,0},{80,16},{96,32},{112,48}... | collective-permute-start | bytes 196616 | tf_op jit(solution)/shard_map/ppermute | solution.py:28
  580.0 8.5 %collective-permute-start.12 = (f32[1,2,16,512]{3,2,0,1:T(8,128)S(1)}, f32[1,2,16,512]{3,2,0,1:T(8,128)S(1)}, u32[]{:S(2)}, u32[]{:S(2)}) collective-permute-start(f32[1,2,16,512]{3,2,0,1:T(8,128)S(1)} %get-tuple-element.48), channel_id=1, source_target_pairs={{0,208},{16,224},{32,240},{48,0},{64,16},{80,32},{96,48},{112,64},... | collective-permute-start | bytes 196616 | tf_op jit(solution)/shard_map/ppermute | solution.py:28
  586.0 7.3 %collective-permute-start.13 = (f32[1,2,16,512]{3,2,0,1:T(8,128)S(1)}, f32[1,2,16,512]{3,2,0,1:T(8,128)S(1)}, u32[]{:S(2)}, u32[]{:S(2)}) collective-permute-start(f32[1,2,16,512]{3,2,0,1:T(8,128)S(1)} %get-tuple-element.47), channel_id=1, source_target_pairs={{0,224},{16,240},{32,0},{48,16},{64,32},{80,48},{96,64},{112,80},{... | collective-permute-start | bytes 196616 | tf_op jit(solution)/shard_map/ppermute | solution.py:28
  586.1 7.2 %collective-permute-start.14 = (f32[1,2,16,512]{3,2,0,1:T(8,128)S(1)}, f32[1,2,16,512]{3,2,0,1:T(8,128)S(1)}, u32[]{:S(2)}, u32[]{:S(2)}) collective-permute-start(f32[1,2,16,512]{3,2,0,1:T(8,128)S(1)} %get-tuple-element.46), channel_id=1, source_target_pairs={{0,240},{16,0},{32,16},{48,32},{64,48},{80,64},{96,80},{112,96},{1... | collective-permute-start | bytes 196616 | tf_op jit(solution)/shard_map/ppermute | solution.py:28
Sparse Core Ops, SparseCore 0:
  141.2 270.1 all-reduce.2
